TPU v7x, 256 devices: a whole 4x4x8 slice. The times are simulated.
256 devices in a mesh: chan: 16 (over z, core), rad: 16 (over y, x).
Axes of the slice: x: 4, y: 4, z: 8, core: 2. Of those that a mesh axis runs over, the one named last changes fastest.
Arguments:
- state: float32 [2048, 2, 16, 1536], P('chan', None, None, 'rad'), may hold values from -200 to 200
- coupling: float32 [64, 16, 4, 32, 32], P('chan'), may hold values from -1.1 to 1.1
- fetch_group: int32 [16, 16], replicated, may hold values from 0 to 3
- live_slots: int32 [64], P('chan'), may hold values from 1 to 16, as said below
- radius_one: float32 [16], replicated, may hold values from 1 to 6
- radius_two: float32 [1536], P('rad'), may hold values from 1 to 6
- kinetic_diag: float32 [12, 128, 128], replicated, may hold values from -2 to 5
- kinetic_link: float32 [11, 128, 128], replicated, may hold values from -0.5 to 0.5
Outputs:
- orthogonal: float32 [2048, 2, 16, 1536], P(('chan', 'rad'))
- arnoldi_coeffs: float32 [3], replicated
Inputs may be any that keep to these rules, and one draw needn't show every extreme that they name: `live_slots`: every draw has a block with all 16 slots live.
All inputs are finite; a program needn't handle non-finite values.
Results may differ from a plain program's by a relative error of at most 0.0003.
Values sent between devices are 32-bit elements; how exact they have to be, the bound alone decides.
A program may use at most 128 MiB of HBM per device.

v0:
```python
import jax
import jax.numpy as jnp
from jax import lax
from jax.sharding import PartitionSpec as P

C = 2048
R = 1536


def radial_kernel(radius_one, radius_two, orders):
    nearer = jnp.minimum(radius_one[:, None], radius_two[None, :])
    farther = jnp.maximum(radius_one[:, None], radius_two[None, :])
    powers = jnp.arange(orders).astype(radius_one.dtype)[:, None, None]
    return nearer[None] ** powers / farther[None] ** (powers + 1.0)


def kinetic(field, kinetic_diag, kinetic_link):
    elements = kinetic_diag.shape[0]
    points = kinetic_diag.shape[1]
    rows = field.reshape(-1, elements, points)
    result = jnp.einsum("rep,eqp->req", rows, kinetic_diag, precision=lax.Precision.HIGHEST)
    lower = jnp.einsum("rep,eqp->req", rows[:, :-1], kinetic_link, precision=lax.Precision.HIGHEST)
    upper = jnp.einsum("rep,epq->req", rows[:, 1:], kinetic_link, precision=lax.Precision.HIGHEST)
    result = (
        result + jnp.pad(lower, ((0, 0), (1, 0), (0, 0))) + jnp.pad(upper, ((0, 0), (0, 1), (0, 0)))
    )
    return result.reshape(field.shape)


def coupling_products(state, coupling, fetch_group, live_slots, radius_one, radius_two):
    chan_count = lax.axis_size("chan")
    my_rank = lax.axis_index("chan")
    local_channels = state.shape[0]
    planes = state.shape[1]
    band = state.shape[2]
    radial = state.shape[3]
    groups_here = coupling.shape[0]
    orders = coupling.shape[2]
    block = coupling.shape[3]
    cells = planes * band * radial
    grouped = state.reshape(groups_here, block, cells)
    outgoing = jnp.take(grouped, fetch_group[:, my_rank], axis=0)
    incoming = lax.all_to_all(outgoing, "chan", split_axis=0, concat_axis=0, tiled=True)
    incoming = incoming.reshape(chan_count * block, cells)
    slot_of = (jnp.arange(chan_count, dtype=jnp.int32) - my_rank) % chan_count
    weights = jnp.take(coupling, slot_of, axis=1)
    active = (slot_of[None, :] < live_slots[:, None]).astype(jnp.float32)
    weights = weights * active[:, :, None, None, None]
    matrices = weights.transpose(2, 0, 3, 1, 4).reshape(orders, local_channels, chan_count * block)
    kernel = radial_kernel(radius_one, radius_two, orders)
    kernel = jnp.broadcast_to(kernel[:, None], (orders, planes, band, radial)).reshape(
        orders, cells
    )
    total = jnp.zeros((local_channels, cells), jnp.float32)
    for order in range(orders):
        product = jnp.dot(
            matrices[order],
            incoming,
            precision=lax.Precision.HIGHEST,
            preferred_element_type=jnp.float32,
        )
        total = total + kernel[order] * product
    return total.reshape(state.shape)


def per_device(
    state, coupling, fetch_group, live_slots, radius_one, radius_two, kinetic_diag, kinetic_link
):
    coupled = coupling_products(state, coupling, fetch_group, live_slots, radius_one, radius_two)
    state_here, coupled_here = (
        lax.all_to_all(state, "rad", split_axis=0, concat_axis=3, tiled=True),
        lax.all_to_all(coupled, "rad", split_axis=0, concat_axis=3, tiled=True),
    )
    applied = kinetic(state_here, kinetic_diag, kinetic_link) + coupled_here
    wave_re = applied[:, 1]
    wave_im = -applied[:, 0]
    state_re = state_here[:, 0]
    state_im = state_here[:, 1]
    total_count = 2.0 * C * state.shape[2] * R
    cross_re = jnp.sum(state_re * wave_re + state_im * wave_im)
    cross_im = jnp.sum(state_re * wave_im - state_im * wave_re)
    self_sq = jnp.sum(state_here * state_here)
    cross_re, cross_im, self_sq = lax.psum((cross_re, cross_im, self_sq), ("chan", "rad"))
    proj_re = cross_re / self_sq
    proj_im = cross_im / self_sq
    orth_re = wave_re - (proj_re * state_re - proj_im * state_im)
    orth_im = wave_im - (proj_re * state_im + proj_im * state_re)
    square_mean = (
        lax.psum(jnp.sum(orth_re * orth_re + orth_im * orth_im), ("chan", "rad")) / total_count
    )
    rms = jnp.sqrt(square_mean + 1e-06)
    orthogonal = jnp.stack([orth_re, orth_im], axis=1)
    return (orthogonal, jnp.stack([proj_re, proj_im, rms]))


def solution(mesh):
    placed = (
        P("chan", None, None, "rad"),
        P("chan", None, None, None, None),
        P(),
        P("chan"),
        P(),
        P("rad"),
        P(),
        P(),
    )
    return jax.shard_map(
        per_device,
        mesh=mesh,
        in_specs=placed,
        out_specs=(P(("chan", "rad"), None, None, None), P()),
        check_vma=False,
    )
```

profile of v0, /device:TPU:1, one launch (start us, length us, event | category | flops | bytes accessed | tf_op | source)
XLA Modules:
  0.0 410.5 jit_solution(6286049403578286027)
XLA Ops:
  2.5 3.0 copy.55
  8.0 3.6 gather_fusion.1
  11.7 6.5 %broadcast_select_fusion = f32[16,32,3072]{2,1,0:T(8,128)} fusion(f32[16,32,3072]{2,1,0:T(8,128)} %gather_fusion.1, pred[16]{0:T(512)(128)(4,1)S(1)} %and_reduce_fusion), kind=kLoop, calls=%fused_computation.11 | loop fusion | flops 1572864 | bytes 12582928 | tf_op jit(solution)/shard_map/jit(_take)/select_n | solution.py:42
  18.1 10.0 %all-to-all-start.1 = ((f32[16,32,3072]{2,1,0:T(8,128)}), f32[16,32,3072]{2,1,0:T(8,128)}, u32[]{:S(2)}, u32[]{:S(2)}) async-start(f32[16,32,3072]{2,1,0:T(8,128)} %broadcast_select_fusion), calls=%async_computation.1 | async-start | bytes 12582912 | tf_op jit(solution)/shard_map/all_to_all | solution.py:43
  28.2 5.0 %gather_fusion = f32[16,4,4,32,32]{4,3,2,1,0:T(8,128)} fusion(f32[4,16,4,32,32]{4,3,2,1,0:T(8,128)} %param.9, s32[1024]{0:T(1024)S(1)} %pad_clamp_fusion.1), kind=kCustom, calls=%fused_computation | custom fusion | bytes 2097216 | tf_op jit(solution)/shard_map/jit(_take)/gather | solution.py:46
  46.3 120.3 %all-to-all-done.1 = f32[16,32,3072]{2,1,0:T(8,128)} async-done(((f32[16,32,3072]{2,1,0:T(8,128)}), f32[16,32,3072]{2,1,0:T(8,128)}, u32[]{:S(2)}, u32[]{:S(2)}) %all-to-all-start.1) | async-done | bytes 6291488 | tf_op jit(solution)/shard_map/all_to_all | solution.py:43
  166.6 6.8 %all-to-all-start = ((f32[128,2,16,96]{3,2,1,0:T(8,128)}), f32[128,2,16,96]{3,2,1,0:T(8,128)S(1)}, u32[]{:S(2)}, u32[]{:S(2)}) async-start(f32[128,2,16,96]{3,2,1,0:T(8,128)} %copy.55), calls=%async_computation | async-start | bytes 4194304 | tf_op jit(solution)/shard_map/all_to_all | solution.py:71
  173.4 5.6 %convolution_multiply_fusion.3 = f32[128,3072]{1,0:T(8,128)S(1)} fusion(f32[128,512]{1,0:T(8,128)S(1)} %squeeze.23, f32[512,3072]{1,0:T(8,128)} %bitcast.8, f32[3072]{0:T(1024)S(1)} %broadcast_in_dim.51), kind=kOutput, calls=%fused_computation.10 | convolution fusion | flops 2416312320 | bytes 8138752 | tf_op jit(solution)/shard_map/dot_general | solution.py:56
  179.0 5.6 %fusion.3 = f32[128,3072]{1,0:T(8,128)S(1)} fusion(f32[128,3072]{1,0:T(8,128)S(1)} %convolution_multiply_fusion.3, f32[128,512]{1,0:T(8,128)S(1)} %squeeze.24, f32[512,3072]{1,0:T(8,128)} %bitcast.8, f32[3072]{0:T(1024)S(1)} %broadcast_in_dim.57), kind=kOutput, calls=%fused_computation.9 | convolution fusion | flops 2416705536 | bytes 9711616 | tf_op jit(solution)/shard_map/dot_general | solution.py:56
  184.6 5.6 %fusion.2 = f32[128,3072]{1,0:T(8,128)S(1)} fusion(f32[128,3072]{1,0:T(8,128)S(1)} %fusion.3, f32[128,512]{1,0:T(8,128)S(1)} %copy-done.6, f32[512,3072]{1,0:T(8,128)} %bitcast.8, f32[3072]{0:T(1024)S(1)} %broadcast_in_dim.59), kind=kOutput, calls=%fused_computation.7 | convolution fusion | flops 2416705536 | bytes 9711616 | tf_op jit(solution)/shard_map/dot_general | solution.py:56
  190.2 7.3 %fusion.1 = f32[128,3072]{1,0:T(8,128)} fusion(f32[128,3072]{1,0:T(8,128)S(1)} %fusion.2, f32[128,512]{1,0:T(8,128)S(1)} %copy-done.7, f32[512,3072]{1,0:T(8,128)} %bitcast.8, f32[3072]{0:T(1024)S(1)} %broadcast_in_dim.61), kind=kOutput, calls=%fused_computation.5 | convolution fusion | flops 2416705536 | bytes 9711616 | tf_op jit(solution)/shard_map/dot_general | solution.py:56
  197.6 3.0 copy.67
  200.6 3.0 copy.68
  204.9 6.7 %all-to-all-start.2 = ((f32[128,2,16,96]{3,2,1,0:T(8,128)}), f32[128,2,16,96]{3,2,1,0:T(8,128)}, u32[]{:S(2)}, u32[]{:S(2)}) async-start(f32[128,2,16,96]{3,2,1,0:T(8,128)} %copy.68), calls=%async_computation.2 | async-start | bytes 4194304 | tf_op jit(solution)/shard_map/all_to_all | solution.py:72
  211.7 2.8 copy.56
  224.8 2.8 fusion.4
  227.6 2.9 copy.61
  230.5 2.6 reshape.225
  233.1 2.7 multiply_reduce_fusion
  235.8 4.0 all-to-all-done.2
  239.8 4.1 %copy.69 = f32[8,2,16,16,96]{4,3,2,1,0:T(8,128)} copy(f32[8,2,16,16,96]{4,2,1,0,3:T(8,128)} %bitcast.14) | data formatting | bytes 3145728 | tf_op jit(solution)/shard_map/all_to_all | solution.py:72
  244.0 3.1 all_to_all.36
  250.3 77.7 %all-reduce.2 = (f32[]{:T(128)}, f32[]{:T(128)}, f32[]{:T(128)}) all-reduce(f32[]{:T(128)} %get-tuple-element.3, f32[]{:T(128)} %multiply_reduce_fusion, f32[]{:T(128)} %get-tuple-element.2), channel_id=1, replica_groups=mesh['chan'=16,'rad'=16] {'chan','rad'}, use_global_device_ids=true, to_apply=%region_5.6 | all-reduce | flops 3 | bytes 24 | tf_op jit(solution)/shard_map/psum | solution.py:83
  334.2 72.6 %psum.31 = f32[]{:T(128)} all-reduce(f32[]{:T(128)} %fusion.13), channel_id=1, replica_groups=mesh['chan'=16,'rad'=16] {'chan','rad'}, use_global_device_ids=true, to_apply=%region_7.8 | all-reduce | flops 1 | bytes 8 | tf_op jit(solution)/shard_map/psum | solution.py:89
  (66 shorter events, 39.0 us)
Async XLA Ops:
  0.6 224.2 %copy-start = (f32[12,128,128]{2,1,0:T(8,128)S(1)}, f32[12,128,128]{2,1,0:T(8,128)}, u32[]{:S(2)}) copy-start(f32[12,128,128]{2,1,0:T(8,128)} %param.14) | copy-start | bytes 2359300
  18.1 148.5 %all-to-all-start.1 = ((f32[16,32,3072]{2,1,0:T(8,128)}), f32[16,32,3072]{2,1,0:T(8,128)}, u32[]{:S(2)}, u32[]{:S(2)}) async-start(f32[16,32,3072]{2,1,0:T(8,128)} %broadcast_select_fusion), calls=%async_computation.1 | async-start | bytes 12582912 | tf_op jit(solution)/shard_map/all_to_all | solution.py:43
  28.2 5.0 %copy-start.8 = (s32[4]{0:T(128)S(1)}, s32[4]{0:T(128)}, u32[]{:S(2)}) copy-start(s32[4]{0:T(128)} %param.11) | copy-start | bytes 52
  37.8 1.1 copy-start.9
  37.8 1.1 copy-start.10
  166.6 37.0 %all-to-all-start = ((f32[128,2,16,96]{3,2,1,0:T(8,128)}), f32[128,2,16,96]{3,2,1,0:T(8,128)S(1)}, u32[]{:S(2)}, u32[]{:S(2)}) async-start(f32[128,2,16,96]{3,2,1,0:T(8,128)} %copy.55), calls=%async_computation | async-start | bytes 4194304 | tf_op jit(solution)/shard_map/all_to_all | solution.py:71
  179.0 5.6 %copy-start.6 = (f32[128,512]{1,0:T(8,128)S(1)}, f32[128,512]{1,0:T(8,128)}, u32[]{:S(2)}) copy-start(f32[128,512]{1,0:T(8,128)} %squeeze.25) | copy-start | bytes 786436
  184.6 5.6 %copy-start.7 = (f32[128,512]{1,0:T(8,128)S(1)}, f32[128,512]{1,0:T(8,128)}, u32[]{:S(2)}) copy-start(f32[128,512]{1,0:T(8,128)} %squeeze.26) | copy-start | bytes 786436
  203.6 1.3 copy-start.4
  204.9 34.9 %all-to-all-start.2 = ((f32[128,2,16,96]{3,2,1,0:T(8,128)}), f32[128,2,16,96]{3,2,1,0:T(8,128)}, u32[]{:S(2)}, u32[]{:S(2)}) async-start(f32[128,2,16,96]{3,2,1,0:T(8,128)} %copy.68), calls=%async_computation.2 | async-start | bytes 4194304 | tf_op jit(solution)/shard_map/all_to_all | solution.py:72
  214.4 1.4 copy-start.3
  219.7 2.2 copy-start.5
  249.1 1.1 copy-start.1
  330.5 2.4 copy-start.2
where the time goes:
time: 412 us; the launch traced here: 410 us
  blocking collectives  150 us (36%)
  waiting for transfers between devices  124 us (30%)
  local copies, waits for them, and re-layouts  54.6 us (13%)
  matrix products  29.7 us (7%)
  other arithmetic  23.9 us (6%)
  starting transfers between devices  23.5 us (6%)
  between operations  4.18 us (1%)
    all_to_all x1, waiting for transfers between devices, coupling_products(): lax.all_to_all(outgoing, 'chan', split_axis=0, concat_axis=0, tiled=True)  120 us
    psum x1, blocking collectives, per_device(): lax.psum((cross_re, cross_im, self_sq), ('chan', 'rad'))  77.7 us
    psum x1, blocking collectives, per_device(): lax.psum(jnp.sum(orth_re * orth_re + orth_im * orth_im), ('chan', 'rad'))  72.6 us
    dot_general x4, matrix products, coupling_products(): jnp.dot(matrices[order], incoming, precision=lax.Precision.HIGHEST, prefe...  24.1 us
    all_to_all x1, starting transfers between devices, coupling_products(): lax.all_to_all(outgoing, 'chan', split_axis=0, concat_axis=0, tiled=True)  9.98 us
  transfers between devices with their start and end apart: 3, of which 2 were waited for; matrix products, arithmetic and copies ran while one was open for 17% of the time, Pallas kernels for 0%

commit v1 on v0

--- a/solution.py
+++ b/solution.py
@@ -5,6 +5,7 @@
 
 C = 2048
 R = 1536
+vector_post = lambda tile_in, link_axis, axis_tag: lax.psum(lax.psum(tile_in, link_axis), axis_tag)
 
 
 def radial_kernel(radius_one, radius_two, orders):
@@ -80,7 +81,7 @@
     cross_re = jnp.sum(state_re * wave_re + state_im * wave_im)
     cross_im = jnp.sum(state_re * wave_im - state_im * wave_re)
     self_sq = jnp.sum(state_here * state_here)
-    cross_re, cross_im, self_sq = lax.psum((cross_re, cross_im, self_sq), ("chan", "rad"))
+    cross_re, cross_im, self_sq = vector_post((cross_re, cross_im, self_sq), "rad", "chan")
     proj_re = cross_re / self_sq
     proj_im = cross_im / self_sq
     orth_re = wave_re - (proj_re * state_re - proj_im * state_im)

time: 412 us -> 398 us (0.966)
  blocking collectives: 150 us -> 136 us
    psum x1 -> x2, blocking collectives: 77.7 us -> 63.7 us  [the longest x1 33.3 us: lax.psum(lax.psum(tile_in, link_axis), axis_tag)]
where the time goes in v1:
time: 398 us; the launch traced here: 397 us
  blocking collectives  136 us (34%)
  waiting for transfers between devices  124 us (31%)
  local copies, waits for them, and re-layouts  54.6 us (14%)
  matrix products  29.7 us (7%)
  other arithmetic  23.9 us (6%)
  starting transfers between devices  23.5 us (6%)
  between operations  4.17 us (1%)
    all_to_all x1, waiting for transfers between devices, coupling_products(): lax.all_to_all(outgoing, 'chan', split_axis=0, concat_axis=0, tiled=True)  120 us
    psum x1, blocking collectives, per_device(): lax.psum(jnp.sum(orth_re * orth_re + orth_im * orth_im), ('chan', 'rad'))  72.8 us
    psum x1, blocking collectives, lax.psum(lax.psum(tile_in, link_axis), axis_tag)  33.3 us
    psum x1, blocking collectives, lax.psum(tile_in, link_axis)  30.3 us
    dot_general x4, matrix products, coupling_products(): jnp.dot(matrices[order], incoming, precision=lax.Precision.HIGHEST, prefe...  24.1 us
    all_to_all x1, starting transfers between devices, coupling_products(): lax.all_to_all(outgoing, 'chan', split_axis=0, concat_axis=0, tiled=True)  9.98 us
  transfers between devices with their start and end apart: 3, of which 2 were waited for; matrix products, arithmetic and copies ran while one was open for 17% of the time, Pallas kernels for 0%

profile of v1, /device:TPU:1, one launch (start us, length us, event | category | flops | bytes accessed | tf_op | source)
XLA Modules:
  0.0 396.6 jit_solution(9500042594376296267)
XLA Ops:
  2.5 3.0 copy.55
  8.0 3.6 gather_fusion.1
  11.7 6.5 %broadcast_select_fusion = f32[16,32,3072]{2,1,0:T(8,128)} fusion(f32[16,32,3072]{2,1,0:T(8,128)} %gather_fusion.1, pred[16]{0:T(512)(128)(4,1)S(1)} %and_reduce_fusion), kind=kLoop, calls=%fused_computation.11 | loop fusion | flops 1572864 | bytes 12582928 | tf_op jit(solution)/shard_map/jit(_take)/select_n | solution.py:43
  18.1 10.0 %all-to-all-start.1 = ((f32[16,32,3072]{2,1,0:T(8,128)}), f32[16,32,3072]{2,1,0:T(8,128)}, u32[]{:S(2)}, u32[]{:S(2)}) async-start(f32[16,32,3072]{2,1,0:T(8,128)} %broadcast_select_fusion), calls=%async_computation.1 | async-start | bytes 12582912 | tf_op jit(solution)/shard_map/all_to_all | solution.py:44
  28.2 5.0 %gather_fusion = f32[16,4,4,32,32]{4,3,2,1,0:T(8,128)} fusion(f32[4,16,4,32,32]{4,3,2,1,0:T(8,128)} %param.9, s32[1024]{0:T(1024)S(1)} %pad_clamp_fusion.1), kind=kCustom, calls=%fused_computation | custom fusion | bytes 2097216 | tf_op jit(solution)/shard_map/jit(_take)/gather | solution.py:47
  46.3 120.3 %all-to-all-done.1 = f32[16,32,3072]{2,1,0:T(8,128)} async-done(((f32[16,32,3072]{2,1,0:T(8,128)}), f32[16,32,3072]{2,1,0:T(8,128)}, u32[]{:S(2)}, u32[]{:S(2)}) %all-to-all-start.1) | async-done | bytes 6291488 | tf_op jit(solution)/shard_map/all_to_all | solution.py:44
  166.6 6.8 %all-to-all-start = ((f32[128,2,16,96]{3,2,1,0:T(8,128)}), f32[128,2,16,96]{3,2,1,0:T(8,128)S(1)}, u32[]{:S(2)}, u32[]{:S(2)}) async-start(f32[128,2,16,96]{3,2,1,0:T(8,128)} %copy.55), calls=%async_computation | async-start | bytes 4194304 | tf_op jit(solution)/shard_map/all_to_all | solution.py:72
  173.4 5.6 %convolution_multiply_fusion.3 = f32[128,3072]{1,0:T(8,128)S(1)} fusion(f32[128,512]{1,0:T(8,128)S(1)} %squeeze.23, f32[512,3072]{1,0:T(8,128)} %bitcast.8, f32[3072]{0:T(1024)S(1)} %broadcast_in_dim.51), kind=kOutput, calls=%fused_computation.10 | convolution fusion | flops 2416312320 | bytes 8138752 | tf_op jit(solution)/shard_map/dot_general | solution.py:57
  179.0 5.6 %fusion.3 = f32[128,3072]{1,0:T(8,128)S(1)} fusion(f32[128,3072]{1,0:T(8,128)S(1)} %convolution_multiply_fusion.3, f32[128,512]{1,0:T(8,128)S(1)} %squeeze.24, f32[512,3072]{1,0:T(8,128)} %bitcast.8, f32[3072]{0:T(1024)S(1)} %broadcast_in_dim.57), kind=kOutput, calls=%fused_computation.9 | convolution fusion | flops 2416705536 | bytes 9711616 | tf_op jit(solution)/shard_map/dot_general | solution.py:57
  184.6 5.6 %fusion.2 = f32[128,3072]{1,0:T(8,128)S(1)} fusion(f32[128,3072]{1,0:T(8,128)S(1)} %fusion.3, f32[128,512]{1,0:T(8,128)S(1)} %copy-done.6, f32[512,3072]{1,0:T(8,128)} %bitcast.8, f32[3072]{0:T(1024)S(1)} %broadcast_in_dim.59), kind=kOutput, calls=%fused_computation.7 | convolution fusion | flops 2416705536 | bytes 9711616 | tf_op jit(solution)/shard_map/dot_general | solution.py:57
  190.2 7.3 %fusion.1 = f32[128,3072]{1,0:T(8,128)} fusion(f32[128,3072]{1,0:T(8,128)S(1)} %fusion.2, f32[128,512]{1,0:T(8,128)S(1)} %copy-done.7, f32[512,3072]{1,0:T(8,128)} %bitcast.8, f32[3072]{0:T(1024)S(1)} %broadcast_in_dim.61), kind=kOutput, calls=%fused_computation.5 | convolution fusion | flops 2416705536 | bytes 9711616 | tf_op jit(solution)/shard_map/dot_general | solution.py:57
  197.6 3.0 copy.67
  200.6 3.0 copy.68
  204.9 6.7 %all-to-all-start.2 = ((f32[128,2,16,96]{3,2,1,0:T(8,128)}), f32[128,2,16,96]{3,2,1,0:T(8,128)}, u32[]{:S(2)}, u32[]{:S(2)}) async-start(f32[128,2,16,96]{3,2,1,0:T(8,128)} %copy.68), calls=%async_computation.2 | async-start | bytes 4194304 | tf_op jit(solution)/shard_map/all_to_all | solution.py:73
  211.7 2.8 copy.56
  224.8 2.8 fusion.4
  227.6 2.9 copy.61
  233.1 2.7 multiply_reduce_fusion
  235.8 4.0 %all-to-all-done.2 = f32[128,2,16,96]{3,2,1,0:T(8,128)} async-done(((f32[128,2,16,96]{3,2,1,0:T(8,128)}), f32[128,2,16,96]{3,2,1,0:T(8,128)}, u32[]{:S(2)}, u32[]{:S(2)}) %all-to-all-start.2) | async-done | bytes 1572896 | tf_op jit(solution)/shard_map/all_to_all | solution.py:73
  239.8 4.1 %copy.69 = f32[8,2,16,16,96]{4,3,2,1,0:T(8,128)} copy(f32[8,2,16,16,96]{4,2,1,0,3:T(8,128)} %bitcast.14) | data formatting | bytes 3145728 | tf_op jit(solution)/shard_map/all_to_all | solution.py:73
  244.0 3.1 all_to_all.36
  250.3 30.3 %all-reduce.2 = (f32[]{:T(128)}, f32[]{:T(128)}, f32[]{:T(128)}) all-reduce(f32[]{:T(128)} %get-tuple-element.3, f32[]{:T(128)} %multiply_reduce_fusion, f32[]{:T(128)} %get-tuple-element.2), channel_id=1, replica_groups=mesh['chan'=16,'rad'=16] {'rad'}, use_global_device_ids=true, to_apply=%region_7.8 | all-reduce | flops 3 | bytes 24 | tf_op jit(solution)/shard_map/psum | solution.py:8
  280.6 33.3 %all-reduce.3 = (f32[]{:T(128)}, f32[]{:T(128)}, f32[]{:T(128)}) all-reduce(f32[]{:T(128)} %get-tuple-element.4, f32[]{:T(128)} %get-tuple-element.5, f32[]{:T(128)} %get-tuple-element.6), channel_id=1, replica_groups=mesh['chan'=16,'rad'=16] {'chan'}, use_global_device_ids=true, to_apply=%region_8.9 | all-reduce | flops 3 | bytes 24 | tf_op jit(solution)/shard_map/psum | solution.py:8
  320.1 72.8 %psum.55 = f32[]{:T(128)} all-reduce(f32[]{:T(128)} %fusion.13), channel_id=1, replica_groups=mesh['chan'=16,'rad'=16] {'chan','rad'}, use_global_device_ids=true, to_apply=%region_10.11 | all-reduce | flops 1 | bytes 8 | tf_op jit(solution)/shard_map/psum | solution.py:90
  (67 shorter events, 41.6 us)
Async XLA Ops:
  0.6 224.2 %copy-start = (f32[12,128,128]{2,1,0:T(8,128)S(1)}, f32[12,128,128]{2,1,0:T(8,128)}, u32[]{:S(2)}) copy-start(f32[12,128,128]{2,1,0:T(8,128)} %param.14) | copy-start | bytes 2359300
  18.1 148.5 %all-to-all-start.1 = ((f32[16,32,3072]{2,1,0:T(8,128)}), f32[16,32,3072]{2,1,0:T(8,128)}, u32[]{:S(2)}, u32[]{:S(2)}) async-start(f32[16,32,3072]{2,1,0:T(8,128)} %broadcast_select_fusion), calls=%async_computation.1 | async-start | bytes 12582912 | tf_op jit(solution)/shard_map/all_to_all | solution.py:44
  28.2 5.0 %copy-start.8 = (s32[4]{0:T(128)S(1)}, s32[4]{0:T(128)}, u32[]{:S(2)}) copy-start(s32[4]{0:T(128)} %param.11) | copy-start | bytes 52
  37.8 1.1 copy-start.9
  37.8 1.1 copy-start.10
  166.6 37.0 %all-to-all-start = ((f32[128,2,16,96]{3,2,1,0:T(8,128)}), f32[128,2,16,96]{3,2,1,0:T(8,128)S(1)}, u32[]{:S(2)}, u32[]{:S(2)}) async-start(f32[128,2,16,96]{3,2,1,0:T(8,128)} %copy.55), calls=%async_computation | async-start | bytes 4194304 | tf_op jit(solution)/shard_map/all_to_all | solution.py:72
  179.0 5.6 %copy-start.6 = (f32[128,512]{1,0:T(8,128)S(1)}, f32[128,512]{1,0:T(8,128)}, u32[]{:S(2)}) copy-start(f32[128,512]{1,0:T(8,128)} %squeeze.25) | copy-start | bytes 786436
  184.6 5.6 %copy-start.7 = (f32[128,512]{1,0:T(8,128)S(1)}, f32[128,512]{1,0:T(8,128)}, u32[]{:S(2)}) copy-start(f32[128,512]{1,0:T(8,128)} %squeeze.26) | copy-start | bytes 786436
  203.6 1.3 copy-start.4
  204.9 34.9 %all-to-all-start.2 = ((f32[128,2,16,96]{3,2,1,0:T(8,128)}), f32[128,2,16,96]{3,2,1,0:T(8,128)}, u32[]{:S(2)}, u32[]{:S(2)}) async-start(f32[128,2,16,96]{3,2,1,0:T(8,128)} %copy.68), calls=%async_computation.2 | async-start | bytes 4194304 | tf_op jit(solution)/shard_map/all_to_all | solution.py:73
  214.4 1.4 copy-start.3
  219.7 2.2 copy-start.5
  249.1 1.1 copy-start.1
  316.5 2.4 copy-start.2
